TPU v7x, 256 devices: a whole 4x4x8 slice. The times are simulated.
256 devices in a mesh: dp: 64 (over y, z, x_lo), fsdp: 4 (over x_hi, core).
Axes of the slice: x: 4 (x_hi: 2, x_lo: 2; x = x_hi * 2 + x_lo), y: 4, z: 8, core: 2. Of those that a mesh axis runs over, the one named last changes fastest.
Arguments:
- picture_tower_inputs: bfloat16 [131072, 1152], P(('dp', 'fsdp')), may hold values from -6 to 6
- caption_tower_inputs: bfloat16 [131072, 1152], P(('dp', 'fsdp')), may hold values from -6 to 6
- halfwidth_parameter_matrix: bfloat16 [1152, 2304], P('fsdp'), may hold values from -0.1875 to 0.1875
- affinity_multiplier: float32 [1], replicated, may hold values from 4 to 12
- affinity_offset: float32 [1], replicated, may hold values from -6 to -2
- precise_parameter_copy: float32 [1152, 2304], P('fsdp', 'dp'), may hold values from -0.125 to 0.125
- gradient_mean_estimate: float32 [1152, 2304], P('fsdp', 'dp'), may hold values from -4 to 4
- gradient_variance_estimate: float32 [1152, 2304], P('fsdp', 'dp'), may hold values from 0.05 to 1
Outputs:
- img_tangent: bfloat16 [131072, 1152], P(('dp', 'fsdp'))
- txt_tangent: bfloat16 [131072, 1152], P(('dp', 'fsdp'))
- new_master: float32 [1152, 2304], P('fsdp', 'dp')
- new_one: float32 [1152, 2304], P('fsdp', 'dp')
- new_two: float32 [1152, 2304], P('fsdp', 'dp')
- new_weights: bfloat16 [1152, 2304], P('fsdp')
All inputs are finite; a program needn't handle non-finite values.
Results may differ from a plain program's by a relative error of at most 0.008.
Values may be sent and summed in bfloat16 or wider, within the bound.
No kernel may reach another device: no remote copies, remote signals or barrier semaphores. Data moves between devices by JAX's collectives and lax.ppermute only.
A program may use at most 128 MiB of HBM per device.

v0:
```python
import jax
import jax.numpy as jnp
from jax import lax
from jax.sharding import PartitionSpec as P

CYCLE = 4


def shifted(value, axis, steps):
    count = lax.axis_size(axis)
    pairs = [(source, (source + steps) % count) for source in range(count)]
    return lax.ppermute(value, axis, pairs)


def normalize(projected):
    inv_norm = lax.rsqrt(jnp.sum(projected * projected, axis=-1, keepdims=True) + 1e-06)
    return (projected * inv_norm, inv_norm)


def contract_rows(left, right):
    return lax.dot_general(
        left, right, (((0,), (0,)), ((), ())), preferred_element_type=jnp.float32
    )


def weigh_pairs(image_rows, text_rows, affinity_multiplier_name, shift_value, sign_label):
    logits = (
        affinity_multiplier_name
        * lax.dot_general(
            image_rows, text_rows, (((1,), (1,)), ((), ())), preferred_element_type=jnp.float32
        )
        + shift_value
    )
    return (-sign_label * jax.nn.sigmoid(-sign_label * logits) * affinity_multiplier_name).astype(
        jnp.bfloat16
    )


def body(
    picture_tower_inputs,
    caption_tower_inputs,
    halfwidth_parameter_matrix,
    affinity_multiplier,
    affinity_offset,
    precise_parameter_copy,
    gradient_mean_estimate,
    gradient_variance_estimate,
):
    row_count = picture_tower_inputs.shape[0]
    feature_width = picture_tower_inputs.shape[1]
    zero_block = jnp.zeros((row_count, feature_width), jnp.float32)
    rows_per_block = lax.all_gather(halfwidth_parameter_matrix, "fsdp", axis=0, tiled=True)
    part_img = picture_tower_inputs
    part_txt = caption_tower_inputs
    proj_img = jnp.dot(
        part_img, rows_per_block[:, :feature_width], preferred_element_type=jnp.float32
    )
    proj_txt = jnp.dot(
        part_txt, rows_per_block[:, feature_width:], preferred_element_type=jnp.float32
    )
    unit_img, norm_img = normalize(proj_img)
    normalized_text, norm_txt = normalize(proj_txt)
    low_img = unit_img.astype(jnp.bfloat16)
    low_txt = normalized_text.astype(jnp.bfloat16)
    affinity_multiplier_name = affinity_multiplier[0]
    shift_value = affinity_offset[0]
    identity_mask = jnp.eye(row_count, dtype=jnp.float32)
    negative_label = -jnp.ones_like(identity_mask)
    visiting = low_txt
    carried = zero_block
    grad_img = zero_block
    for cycle_step in range(CYCLE):
        if cycle_step > 0:
            visiting = shifted(visiting, "dp", 1)
            carried = shifted(carried, "dp", 1)
        if cycle_step == 0:
            sign_label = 2.0 * identity_mask - 1.0
        else:
            sign_label = negative_label
        pair_weight = weigh_pairs(
            low_img, visiting, affinity_multiplier_name, shift_value, sign_label
        )
        grad_img = grad_img + jnp.dot(pair_weight, visiting, preferred_element_type=jnp.float32)
        carried = carried + contract_rows(pair_weight, low_img)
    grad_txt = shifted(carried, "dp", 1 - CYCLE)
    img_tangent = (
        norm_img * (grad_img - unit_img * jnp.sum(unit_img * grad_img, axis=1, keepdims=True))
    ).astype(jnp.bfloat16)
    txt_tangent = (
        norm_txt
        * (grad_txt - normalized_text * jnp.sum(normalized_text * grad_txt, axis=1, keepdims=True))
    ).astype(jnp.bfloat16)
    part_img = picture_tower_inputs
    part_txt = caption_tower_inputs
    owned_rows = lax.psum_scatter(
        jnp.concatenate(
            [contract_rows(part_img, img_tangent), contract_rows(part_txt, txt_tangent)], axis=1
        ).astype(jnp.bfloat16),
        "fsdp",
        scatter_dimension=0,
        tiled=True,
    ).astype(jnp.float32)
    gradient = lax.psum_scatter(owned_rows, "dp", scatter_dimension=1, tiled=True)
    new_one = 0.9 * gradient_mean_estimate + 0.1 * gradient
    new_two = 0.95 * gradient_variance_estimate + 0.05 * gradient * gradient
    new_master = precise_parameter_copy - 0.001 * (
        new_one / (jnp.sqrt(new_two) + 1e-08) + 0.1 * precise_parameter_copy
    )
    new_weights = lax.all_gather(new_master.astype(jnp.bfloat16), "dp", axis=1, tiled=True)
    return (img_tangent, txt_tangent, new_master, new_one, new_two, new_weights)


def solution(mesh):
    return jax.shard_map(
        body,
        mesh=mesh,
        in_specs=(
            P(("dp", "fsdp"), None),
            P(("dp", "fsdp"), None),
            P("fsdp", None),
            P(),
            P(),
            P("fsdp", "dp"),
            P("fsdp", "dp"),
            P("fsdp", "dp"),
        ),
        out_specs=(
            P(("dp", "fsdp"), None),
            P(("dp", "fsdp"), None),
            P("fsdp", "dp"),
            P("fsdp", "dp"),
            P("fsdp", "dp"),
            P("fsdp", None),
        ),
        check_vma=False,
    )
```

profile of v0, /device:TPU:4, one launch (start us, length us, event | category | flops | bytes accessed | tf_op | source)
XLA Modules:
  0.0 1053.1 jit_solution(14474370178524340292)
XLA Ops:
  7.2 0.7 all-gather.4.cloned.1.call-update
  9.3 48.2 %all-gather.4.cloned.1.call-done = bf16[1152,2304]{1,0:T(8,128)(2,1)} async-done(((bf16[288,2304]{1,0:T(8,128)(2,1)}), bf16[1152,2304]{1,0:T(8,128)(2,1)}) %all-gather.4.cloned.1.call-update) | async-done | bytes 5308432 | tf_op jit(solution)/shard_map/all_gather | solution.py:52
  57.5 3.8 multiply_reduce_fusion.3
  61.4 1.9 multiply_reduce_fusion.2
  63.3 0.2 multiply_convert_fusion.3
  63.5 0.2 multiply_convert_fusion.2
  63.7 1.1 fusion.33
  64.8 0.9 fusion.40
  65.7 2.4 collective-permute-start.3
  68.0 0.9 collective-permute-start
  69.0 80.9 %collective-permute-done = bf16[512,1152]{1,0:T(8,128)(2,1)S(1)} collective-permute-done((bf16[512,1152]{1,0:T(8,128)(2,1)S(1)}, bf16[512,1152]{1,0:T(8,128)(2,1)S(1)}, u32[]{:S(2)}, u32[]{:S(2)}) %collective-permute-start) | collective-permute-done | bytes 1179680 | tf_op jit(solution)/shard_map/ppermute | solution.py:12
  149.9 1.0 fusion.36
  150.9 0.9 convolution_add_fusion
  151.8 0.1 collective-permute-start.4
  151.9 0.1 collective-permute-start.1
  152.0 82.2 %collective-permute-done.1 = bf16[512,1152]{1,0:T(8,128)(2,1)S(1)} collective-permute-done((bf16[512,1152]{1,0:T(8,128)(2,1)S(1)}, bf16[512,1152]{1,0:T(8,128)(2,1)S(1)}, u32[]{:S(2)}, u32[]{:S(2)}) %collective-permute-start.1) | collective-permute-done | bytes 1179680 | tf_op jit(solution)/shard_map/ppermute | solution.py:12
  234.2 1.0 fusion.35
  235.2 0.9 fusion.41
  236.1 0.2 add.99
  236.4 0.3 collective-permute-start.5
  236.7 81.4 %collective-permute-done.2 = bf16[512,1152]{1,0:T(8,128)(2,1)S(1)} collective-permute-done((bf16[512,1152]{1,0:T(8,128)(2,1)S(1)}, bf16[512,1152]{1,0:T(8,128)(2,1)S(1)}, u32[]{:S(2)}, u32[]{:S(2)}) %collective-permute-start.2) | collective-permute-done | bytes 1179680 | tf_op jit(solution)/shard_map/ppermute | solution.py:12
  318.1 1.0 fusion.34
  319.1 0.9 fusion.42
  320.0 0.2 add.100
  320.2 0.1 collective-permute-start.6
  320.3 0.8 fusion.39
  321.2 0.8 convolution_add_fusion.3
  322.0 0.9 convolution_add_fusion.2
  322.9 1.1 multiply_reduce_fusion.1
  324.0 0.4 multiply_convert_fusion.1
  324.4 1.7 fusion.1
  326.2 85.0 %collective-permute-done.6 = f32[512,1152]{1,0:T(8,128)S(1)} collective-permute-done((f32[512,1152]{1,0:T(8,128)S(1)}, f32[512,1152]{1,0:T(8,128)S(1)}, u32[]{:S(2)}, u32[]{:S(2)}) %collective-permute-start.6) | collective-permute-done | bytes 2359328 | tf_op jit(solution)/shard_map/ppermute | solution.py:12
  411.2 0.4 multiply_reduce_fusion
  411.6 0.4 multiply_convert_fusion
  412.0 1.0 copy-done.2
  413.0 1.7 fusion.2
  414.8 2.8 pad_maximum_fusion
  417.5 8.6 copy.17
  426.2 68.9 %reduce-scatter.6.cloned.1.call-done = bf16[288,2304]{1,0:T(8,128)(2,1)} async-done(((bf16[1152,2304]{1,0:T(8,128)(2,1)}), bf16[288,2304]{1,0:T(8,128)(2,1)}) %reduce-scatter.6.cloned.1.call-update) | async-done | bytes 1327120
  495.1 1.9 copy.18
  497.0 2.0 convert_element_type.40
  499.0 187.4 %fusion = f32[288,48]{0,1:T(8,128)S(1)} fusion(f32[288,2304]{0,1:T(8,128)} %convert_element_type.40), kind=kCustom, calls=%all-reduce-scatter | all-reduce-scatter fusion | flops 884737 | bytes 2710528
  686.4 1.3 collective-permute-start.22
  687.7 1.3 collective-permute-start.21
  689.0 1.3 collective-permute-start.20
  690.3 1.3 collective-permute-start.19
  691.6 1.5 collective-permute-start.18
  693.2 1.3 collective-permute-start.17
  694.5 12.9 %collective-permute-start.16 = (f32[288,48]{0,1:T(8,128)S(1)}, f32[288,48]{0,1:T(8,128)S(1)}, u32[]{:S(2)}, u32[]{:S(2)}) collective-permute-start(f32[288,48]{0,1:T(8,128)S(1)} %fusion), channel_id=1, source_target_pairs={{0,40},{4,44},{8,48},{12,52},{16,56},{20,60},{24,64},{28,68},{32,7... | collective-permute-start | bytes 165896
  707.4 2.5 collective-permute-start.15
  710.0 5.2 collective-permute-start.14
  715.2 2.2 collective-permute-start.13
  717.4 3.4 collective-permute-start.12
  720.8 4.0 collective-permute-start.11
  724.8 3.0 collective-permute-start.10
  727.8 3.3 collective-permute-start.9
  731.2 1.4 collective-permute-start.8
  732.6 4.0 collective-permute-start.7
  736.6 0.6 dynamic-slice.4
  738.0 4.1 concatenate.5
  742.1 1.6 convert_bitcast_fusion
  743.7 298.5 %all-gather.6.cloned.1.call-done = bf16[64,36,288]{2,1,0:T(8,128)(2,1)} async-done(((bf16[1,36,288]{2,1,0:T(8,128)(2,1)}), bf16[64,36,288]{2,1,0:T(8,128)(2,1)}) %all-gather.6.cloned.1.call-update) | async-done | bytes 1327120 | tf_op jit(solution)/shard_map/all_gather | solution.py:109
  1042.2 2.8 reshape.27
  1045.0 1.6 copy.16
  (41 shorter events, 0.4 us)
Async XLA Ops:
  7.2 50.3 %copy-start = (bf16[512,1152]{1,0:T(8,128)(2,1)S(1)}, bf16[512,1152]{1,0:T(8,128)(2,1)}, u32[]{:S(2)}) copy-start(bf16[512,1152]{1,0:T(8,128)(2,1)} %param.8) | copy-start | bytes 3538948
  7.2 50.3 %all-gather.4.cloned.1.call-start = ((), (), s32[]{:S(2)}) async-start(), calls=%async_computation.1 | async-start | bytes 6635520 | tf_op jit(solution)/shard_map/all_gather | solution.py:52
  7.9 487.1 %reduce-scatter.6.cloned.1.call-start = ((), (), s32[]{:S(2)}) async-start(), calls=%async_computation.3 | async-start | bytes 6635520
  9.3 52.1 %copy-start.6 = (bf16[512,1152]{1,0:T(8,128)(2,1)S(1)}, bf16[512,1152]{1,0:T(8,128)(2,1)}, u32[]{:S(2)}) copy-start(bf16[512,1152]{1,0:T(8,128)(2,1)} %param.9) | copy-start | bytes 3538948
  57.5 3.9 copy-start.5
  65.7 85.2 %collective-permute-start.3 = (f32[512,1152]{1,0:T(8,128)S(1)}, f32[512,1152]{1,0:T(8,128)S(1)}, u32[]{:S(2)}, u32[]{:S(2)}) collective-permute-start(f32[512,1152]{1,0:T(8,128)S(1)} %fusion.40), channel_id=1, source_target_pairs={{0,4},{4,8},{8,12},{12,16},{16,20},{20,24},{24,28},{28,32},{32,36}... | collective-permute-start | bytes 7077896 | tf_op jit(solution)/shard_map/ppermute | solution.py:12
  68.0 81.9 %collective-permute-start = (bf16[512,1152]{1,0:T(8,128)(2,1)S(1)}, bf16[512,1152]{1,0:T(8,128)(2,1)S(1)}, u32[]{:S(2)}, u32[]{:S(2)}) collective-permute-start(bf16[512,1152]{1,0:T(8,128)(2,1)S(1)} %multiply_convert_fusion.2), channel_id=1, source_target_pairs={{0,4},{4,8},{8,12},{12,16},{16,20},{20,24},{24,28},{28,32},{32,36}... | collective-permute-start | bytes 3538952 | tf_op jit(solution)/shard_map/ppermute | solution.py:12
  151.8 84.3 %collective-permute-start.4 = (f32[512,1152]{1,0:T(8,128)S(1)}, f32[512,1152]{1,0:T(8,128)S(1)}, u32[]{:S(2)}, u32[]{:S(2)}) collective-permute-start(f32[512,1152]{1,0:T(8,128)S(1)} %convolution_add_fusion), channel_id=1, source_target_pairs={{0,4},{4,8},{8,12},{12,16},{16,20},{20,24},{24,28},{28,32},{32,36}... | collective-permute-start | bytes 7077896 | tf_op jit(solution)/shard_map/ppermute | solution.py:12
  151.9 82.3 %collective-permute-start.1 = (bf16[512,1152]{1,0:T(8,128)(2,1)S(1)}, bf16[512,1152]{1,0:T(8,128)(2,1)S(1)}, u32[]{:S(2)}, u32[]{:S(2)}) collective-permute-start(bf16[512,1152]{1,0:T(8,128)(2,1)S(1)} %collective-permute-done), channel_id=1, source_target_pairs={{0,4},{4,8},{8,12},{12,16},{16,20},{20,24},{24,28},{28,32},{32,36}... | collective-permute-start | bytes 3538952 | tf_op jit(solution)/shard_map/ppermute | solution.py:12
  236.4 83.6 %collective-permute-start.5 = (f32[512,1152]{1,0:T(8,128)S(1)}, f32[512,1152]{1,0:T(8,128)S(1)}, u32[]{:S(2)}, u32[]{:S(2)}) collective-permute-start(f32[512,1152]{1,0:T(8,128)S(1)} %add.99), channel_id=1, source_target_pairs={{0,4},{4,8},{8,12},{12,16},{16,20},{20,24},{24,28},{28,32},{32,36}... | collective-permute-start | bytes 7077896 | tf_op jit(solution)/shard_map/ppermute | solution.py:12
  236.6 81.5 %collective-permute-start.2 = (bf16[512,1152]{1,0:T(8,128)(2,1)S(1)}, bf16[512,1152]{1,0:T(8,128)(2,1)S(1)}, u32[]{:S(2)}, u32[]{:S(2)}) collective-permute-start(bf16[512,1152]{1,0:T(8,128)(2,1)S(1)} %collective-permute-done.1), channel_id=1, source_target_pairs={{0,4},{4,8},{8,12},{12,16},{16,20},{20,24},{24,28},{28,32},{32,36}... | collective-permute-start | bytes 3538952 | tf_op jit(solution)/shard_map/ppermute | solution.py:12
  320.2 91.0 %collective-permute-start.6 = (f32[512,1152]{1,0:T(8,128)S(1)}, f32[512,1152]{1,0:T(8,128)S(1)}, u32[]{:S(2)}, u32[]{:S(2)}) collective-permute-start(f32[512,1152]{1,0:T(8,128)S(1)} %add.100), channel_id=1, source_target_pairs={{0,244},{4,248},{8,252},{12,0},{16,4},{20,8},{24,12},{28,16},{32,2... | collective-permute-start | bytes 7077896 | tf_op jit(solution)/shard_map/ppermute | solution.py:12
  324.4 1.8 copy-start.1
  412.0 1.0 copy-start.2
  426.1 616.1 %all-gather.6.cloned.1.call-start = ((), (), s32[]{:S(2)}) async-start(), calls=%async_computation.2 | async-start | bytes 1996800 | tf_op jit(solution)/shard_map/all_gather | solution.py:109
  499.0 237.7 %copy-start.4 = (u32[256]{0:T(256)S(1)}, u32[256]{0:T(256)}, u32[]{:S(2)}) copy-start(u32[256]{0:T(256)} %constant.28) | copy-start | bytes 3076
  686.4 6.7 collective-permute-start.22
  687.7 6.8 collective-permute-start.21
  689.0 18.4 %collective-permute-start.20 = (f32[288,48]{0,1:T(8,128)S(1)}, f32[288,48]{0,1:T(8,128)S(1)}, u32[]{:S(2)}, u32[]{:S(2)}) collective-permute-start(f32[288,48]{0,1:T(8,128)S(1)} %fusion), channel_id=1, source_target_pairs={{0,56},{4,60},{8,64},{12,68},{16,72},{20,76},{24,80},{28,84},{32,8... | collective-permute-start | bytes 165896
  690.3 19.6 %collective-permute-start.19 = (f32[288,48]{0,1:T(8,128)S(1)}, f32[288,48]{0,1:T(8,128)S(1)}, u32[]{:S(2)}, u32[]{:S(2)}) collective-permute-start(f32[288,48]{0,1:T(8,128)S(1)} %fusion), channel_id=1, source_target_pairs={{0,52},{4,56},{8,60},{12,64},{16,68},{20,72},{24,76},{28,80},{32,8... | collective-permute-start | bytes 165896
  691.6 23.5 %collective-permute-start.18 = (f32[288,48]{0,1:T(8,128)S(1)}, f32[288,48]{0,1:T(8,128)S(1)}, u32[]{:S(2)}, u32[]{:S(2)}) collective-permute-start(f32[288,48]{0,1:T(8,128)S(1)} %fusion), channel_id=1, source_target_pairs={{0,48},{4,52},{8,56},{12,60},{16,64},{20,68},{24,72},{28,76},{32,8... | collective-permute-start | bytes 165896
  693.1 39.5 %copy-start.3 = (f32[288,36]{0,1:T(8,128)}, f32[288,36]{0,1:T(8,128)S(1)}, u32[]{:S(2)}) copy-start(f32[288,36]{0,1:T(8,128)S(1)} %collective-permute-done.22) | copy-start | bytes 124420
  693.2 24.2 %collective-permute-start.17 = (f32[288,48]{0,1:T(8,128)S(1)}, f32[288,48]{0,1:T(8,128)S(1)}, u32[]{:S(2)}, u32[]{:S(2)}) collective-permute-start(f32[288,48]{0,1:T(8,128)S(1)} %fusion), channel_id=1, source_target_pairs={{0,44},{4,48},{8,52},{12,56},{16,60},{20,64},{24,68},{28,72},{32,7... | collective-permute-start | bytes 165896
  694.5 26.3 %collective-permute-start.16 = (f32[288,48]{0,1:T(8,128)S(1)}, f32[288,48]{0,1:T(8,128)S(1)}, u32[]{:S(2)}, u32[]{:S(2)}) collective-permute-start(f32[288,48]{0,1:T(8,128)S(1)} %fusion), channel_id=1, source_target_pairs={{0,40},{4,44},{8,48},{12,52},{16,56},{20,60},{24,64},{28,68},{32,7... | collective-permute-start | bytes 165896
  707.4 17.4 %collective-permute-start.15 = (f32[288,48]{0,1:T(8,128)S(1)}, f32[288,48]{0,1:T(8,128)S(1)}, u32[]{:S(2)}, u32[]{:S(2)}) collective-permute-start(f32[288,48]{0,1:T(8,128)S(1)} %fusion), channel_id=1, source_target_pairs={{0,36},{4,40},{8,44},{12,48},{16,52},{20,56},{24,60},{28,64},{32,6... | collective-permute-start | bytes 165896
  710.0 17.9 %collective-permute-start.14 = (f32[288,48]{0,1:T(8,128)S(1)}, f32[288,48]{0,1:T(8,128)S(1)}, u32[]{:S(2)}, u32[]{:S(2)}) collective-permute-start(f32[288,48]{0,1:T(8,128)S(1)} %fusion), channel_id=1, source_target_pairs={{0,32},{4,36},{8,40},{12,44},{16,48},{20,52},{24,56},{28,60},{32,6... | collective-permute-start | bytes 165896
  715.2 16.0 %collective-permute-start.13 = (f32[288,48]{0,1:T(8,128)S(1)}, f32[288,48]{0,1:T(8,128)S(1)}, u32[]{:S(2)}, u32[]{:S(2)}) collective-permute-start(f32[288,48]{0,1:T(8,128)S(1)} %fusion), channel_id=1, source_target_pairs={{0,28},{4,32},{8,36},{12,40},{16,44},{20,48},{24,52},{28,56},{32,6... | collective-permute-start | bytes 165896
  717.4 15.2 %collective-permute-start.12 = (f32[288,48]{0,1:T(8,128)S(1)}, f32[288,48]{0,1:T(8,128)S(1)}, u32[]{:S(2)}, u32[]{:S(2)}) collective-permute-start(f32[288,48]{0,1:T(8,128)S(1)} %fusion), channel_id=1, source_target_pairs={{0,24},{4,28},{8,32},{12,36},{16,40},{20,44},{24,48},{28,52},{32,5... | collective-permute-start | bytes 165896
  720.8 17.1 %collective-permute-start.11 = (f32[288,48]{0,1:T(8,128)S(1)}, f32[288,48]{0,1:T(8,128)S(1)}, u32[]{:S(2)}, u32[]{:S(2)}) collective-permute-start(f32[288,48]{0,1:T(8,128)S(1)} %fusion), channel_id=1, source_target_pairs={{0,20},{4,24},{8,28},{12,32},{16,36},{20,40},{24,44},{28,48},{32,5... | collective-permute-start | bytes 165896
  724.8 13.1 %collective-permute-start.10 = (f32[288,48]{0,1:T(8,128)S(1)}, f32[288,48]{0,1:T(8,128)S(1)}, u32[]{:S(2)}, u32[]{:S(2)}) collective-permute-start(f32[288,48]{0,1:T(8,128)S(1)} %fusion), channel_id=1, source_target_pairs={{0,16},{4,20},{8,24},{12,28},{16,32},{20,36},{24,40},{28,44},{32,4... | collective-permute-start | bytes 165896
  727.8 10.1 collective-permute-start.9
  731.2 6.7 collective-permute-start.8
  732.6 5.3 collective-permute-start.7
Sparse Core Ops, SparseCore 0:
  9.8 47.6 all-gather.3
  426.2 68.7 reduce-scatter.5
  743.8 298.3 all-gather.5
where the time goes:
time: 1050 us
  waiting for transfers between devices  746 us (71%)
  blocking collectives  187 us (18%)
  starting transfers between devices  54 us (5%)
  local copies, waits for them, and re-layouts  20.6 us (2%)
  matrix products  20.5 us (2%)
  between operations  16.3 us (2%)
    ppermute x7, waiting for transfers between devices, shifted(): return lax.ppermute(value, axis, pairs)  329 us
    all_gather x1, waiting for transfers between devices, body(): lax.all_gather(new_master.astype(jnp.bfloat16), 'dp', axis=1, tiled=True)  299 us
    unnamed x1, blocking collectives  187 us
    unnamed x20, waiting for transfers between devices  69.7 us
    unnamed x17, starting transfers between devices  50 us
    all_gather x1, waiting for transfers between devices, body(): lax.all_gather(halfwidth_parameter_matrix, 'fsdp', axis=0, tiled=True)  48.2 us
  transfers between devices with their start and end apart: 26, of which 8 were waited for; matrix products, arithmetic and copies ran while one was open for 1% of the time, Pallas kernels for 0%

commit v1 on v0

--- a/solution.py
+++ b/solution.py
@@ -106,7 +106,12 @@
     new_master = precise_parameter_copy - 0.001 * (
         new_one / (jnp.sqrt(new_two) + 1e-08) + 0.1 * precise_parameter_copy
     )
-    new_weights = lax.all_gather(new_master.astype(jnp.bfloat16), "dp", axis=1, tiled=True)
+    new_weights = jnp.concatenate(
+        lax.all_to_all(
+            jnp.stack([new_master.astype(jnp.bfloat16)] * lax.axis_size("dp")), "dp", 0, 0
+        ),
+        axis=1,
+    )
     return (img_tangent, txt_tangent, new_master, new_one, new_two, new_weights)
 
 

time: 1050 us -> 803 us (0.76)
  waiting for transfers between devices: 746 us -> 448 us
  blocking collectives: 187 us -> 232 us
    all_gather x1 -> x0, waiting for transfers between devices: 299 us -> none  [body(): lax.all_gather(new_master.astype(jnp.bfloat16), 'dp', axis=1, tiled=True)]
    all_to_all x0 -> x1, blocking collectives: none -> 43.8 us  [body(): lax.all_to_all(jnp.stack([new_master.astype(jnp.bfloat16)] * lax.axis_siz...]
    unnamed x20 -> x19, waiting for transfers between devices: 69.7 us -> 70.2 us
  transfers between devices with their start and end apart: 26 -> 25, of which waited for: 8 -> 7; matrix products, arithmetic and copies ran while one was open for 1% -> 1% of each run, Pallas kernels for 0% -> 0%
where the time goes in v1:
time: 803 us; the launch traced here: 800 us
  waiting for transfers between devices  448 us (56%)
  blocking collectives  232 us (29%)
  starting transfers between devices  54.2 us (7%)
  local copies, waits for them, and re-layouts  20.7 us (3%)
  matrix products  20.5 us (3%)
  between operations  16.5 us (2%)
  other arithmetic  8.5 us (1%)
    ppermute x7, waiting for transfers between devices, shifted(): return lax.ppermute(value, axis, pairs)  330 us
    unnamed x1, blocking collectives  188 us
    unnamed x19, waiting for transfers between devices  70.2 us
    unnamed x17, starting transfers between devices  50.2 us
    all_gather x1, waiting for transfers between devices, body(): lax.all_gather(halfwidth_parameter_matrix, 'fsdp', axis=0, tiled=True)  48.2 us
    all_to_all x1, blocking collectives, body(): lax.all_to_all(jnp.stack([new_master.astype(jnp.bfloat16)] * lax.axis_siz...  43.8 us
    unnamed x20, local copies, waits for them, and re-layouts  18.8 us
  transfers between devices with their start and end apart: 25, of which 7 were waited for; matrix products, arithmetic and copies ran while one was open for 1% of the time, Pallas kernels for 0%

profile of v1, /device:TPU:4, one launch (start us, length us, event | category | flops | bytes accessed | tf_op | source)
XLA Modules:
  0.0 800.4 jit_solution(4183265258245417102)
XLA Ops:
  7.2 0.7 all-gather.2.cloned.1.call-update
  9.3 48.2 %all-gather.2.cloned.1.call-done = bf16[1152,2304]{1,0:T(8,128)(2,1)} async-done(((bf16[288,2304]{1,0:T(8,128)(2,1)}), bf16[1152,2304]{1,0:T(8,128)(2,1)}) %all-gather.2.cloned.1.call-update) | async-done | bytes 5308432 | tf_op jit(solution)/shard_map/all_gather | solution.py:52
  57.5 3.8 multiply_reduce_fusion.3
  61.4 1.9 multiply_reduce_fusion.2
  63.3 0.2 multiply_convert_fusion.3
  63.5 0.2 multiply_convert_fusion.2
  63.7 1.1 fusion.33
  64.8 0.9 fusion.41
  65.7 2.4 collective-permute-start.3
  68.0 0.9 collective-permute-start
  69.0 80.9 %collective-permute-done = bf16[512,1152]{1,0:T(8,128)(2,1)S(1)} collective-permute-done((bf16[512,1152]{1,0:T(8,128)(2,1)S(1)}, bf16[512,1152]{1,0:T(8,128)(2,1)S(1)}, u32[]{:S(2)}, u32[]{:S(2)}) %collective-permute-start) | collective-permute-done | bytes 1179680 | tf_op jit(solution)/shard_map/ppermute | solution.py:12
  149.9 1.0 fusion.36
  150.9 0.9 convolution_add_fusion
  152.0 82.2 %collective-permute-done.1 = bf16[512,1152]{1,0:T(8,128)(2,1)S(1)} collective-permute-done((bf16[512,1152]{1,0:T(8,128)(2,1)S(1)}, bf16[512,1152]{1,0:T(8,128)(2,1)S(1)}, u32[]{:S(2)}, u32[]{:S(2)}) %collective-permute-start.1) | collective-permute-done | bytes 1179680 | tf_op jit(solution)/shard_map/ppermute | solution.py:12
  234.2 1.0 fusion.35
  235.2 0.9 fusion.42
  236.1 0.2 add.99
  236.4 0.3 collective-permute-start.5
  236.7 81.4 %collective-permute-done.2 = bf16[512,1152]{1,0:T(8,128)(2,1)S(1)} collective-permute-done((bf16[512,1152]{1,0:T(8,128)(2,1)S(1)}, bf16[512,1152]{1,0:T(8,128)(2,1)S(1)}, u32[]{:S(2)}, u32[]{:S(2)}) %collective-permute-start.2) | collective-permute-done | bytes 1179680 | tf_op jit(solution)/shard_map/ppermute | solution.py:12
  318.1 1.0 fusion.34
  319.1 0.9 fusion.43
  320.0 0.2 add.100
  320.2 0.1 collective-permute-start.6
  320.3 0.8 fusion.40
  321.2 0.9 convolution_add_fusion.3
  322.0 0.9 convolution_add_fusion.2
  322.9 1.1 multiply_reduce_fusion.1
  324.0 0.4 multiply_convert_fusion.1
  324.4 1.7 fusion.1
  326.2 85.0 %collective-permute-done.6 = f32[512,1152]{1,0:T(8,128)S(1)} collective-permute-done((f32[512,1152]{1,0:T(8,128)S(1)}, f32[512,1152]{1,0:T(8,128)S(1)}, u32[]{:S(2)}, u32[]{:S(2)}) %collective-permute-start.6) | collective-permute-done | bytes 2359328 | tf_op jit(solution)/shard_map/ppermute | solution.py:12
  411.2 0.4 multiply_reduce_fusion
  411.6 0.4 multiply_convert_fusion
  412.0 1.0 copy-done.2
  413.0 1.7 fusion.2
  414.8 2.8 pad_maximum_fusion
  417.6 8.6 %copy.17 = bf16[1152,2304]{1,0:T(8,128)(2,1)} copy(bf16[1152,2304]{0,1:T(8,128)(2,1)} %pad_maximum_fusion) | data formatting | bytes 10616832
  426.1 68.9 %reduce-scatter.6.cloned.1.call-done = bf16[288,2304]{1,0:T(8,128)(2,1)} async-done(((bf16[1152,2304]{1,0:T(8,128)(2,1)}), bf16[288,2304]{1,0:T(8,128)(2,1)}) %reduce-scatter.6.cloned.1.call-update) | async-done | bytes 1327120
  495.1 1.9 copy.18
  497.0 2.0 convert_element_type.40
  499.0 188.3 %fusion = f32[288,48]{0,1:T(8,128)S(1)} fusion(f32[288,2304]{0,1:T(8,128)} %convert_element_type.40), kind=kCustom, calls=%all-reduce-scatter | all-reduce-scatter fusion | flops 884737 | bytes 2710528
  687.3 1.3 collective-permute-start.22
  688.6 1.3 collective-permute-start.21
  690.0 1.3 collective-permute-start.20
  691.3 1.3 collective-permute-start.19
  692.6 1.5 collective-permute-start.18
  694.1 1.3 collective-permute-start.17
  695.4 12.9 %collective-permute-start.16 = (f32[288,48]{0,1:T(8,128)S(1)}, f32[288,48]{0,1:T(8,128)S(1)}, u32[]{:S(2)}, u32[]{:S(2)}) collective-permute-start(f32[288,48]{0,1:T(8,128)S(1)} %fusion), channel_id=1, source_target_pairs={{0,40},{4,44},{8,48},{12,52},{16,56},{20,60},{24,64},{28,68},{32,7... | collective-permute-start | bytes 165896
  708.3 2.5 collective-permute-start.15
  710.9 5.4 collective-permute-start.14
  716.3 2.0 collective-permute-start.13
  718.3 3.6 collective-permute-start.12
  721.9 3.8 collective-permute-start.11
  725.7 3.0 collective-permute-start.10
  728.8 3.3 collective-permute-start.9
  732.1 1.4 collective-permute-start.8
  733.6 4.2 collective-permute-start.7
  737.8 0.6 dynamic-slice.4
  739.1 0.5 collective-permute-done.7
  739.6 4.1 concatenate.5
  743.7 1.6 fusion.38
  745.3 0.2 stack.2
  745.4 43.8 %all_to_all.5 = bf16[64,288,36]{1,2,0:T(8,128)(2,1)S(1)} all-to-all(bf16[64,288,36]{1,2,0:T(8,128)(2,1)S(1)} %stack.2), channel_id=1, replica_groups=mesh['dp'=64,'fsdp'=4] {'dp'}, dimensions={0} | all-to-all | bytes 2654208 | tf_op jit(solution)/shard_map/all_to_all | solution.py:110
  789.3 1.8 reshape.35
  791.0 2.6 copy.16
  (40 shorter events, 0.4 us)
Async XLA Ops:
  7.2 50.3 %copy-start = (bf16[512,1152]{1,0:T(8,128)(2,1)S(1)}, bf16[512,1152]{1,0:T(8,128)(2,1)}, u32[]{:S(2)}) copy-start(bf16[512,1152]{1,0:T(8,128)(2,1)} %param.8) | copy-start | bytes 3538948
  7.2 50.3 %all-gather.2.cloned.1.call-start = ((), (), s32[]{:S(2)}) async-start(), calls=%async_computation.2 | async-start | bytes 6635520 | tf_op jit(solution)/shard_map/all_gather | solution.py:52
  7.9 487.2 %reduce-scatter.6.cloned.1.call-start = ((), (), s32[]{:S(2)}) async-start(), calls=%async_computation.3 | async-start | bytes 6635520
  9.3 52.1 %copy-start.6 = (bf16[512,1152]{1,0:T(8,128)(2,1)S(1)}, bf16[512,1152]{1,0:T(8,128)(2,1)}, u32[]{:S(2)}) copy-start(bf16[512,1152]{1,0:T(8,128)(2,1)} %param.9) | copy-start | bytes 3538948
  57.5 3.9 copy-start.5
  65.7 85.2 %collective-permute-start.3 = (f32[512,1152]{1,0:T(8,128)S(1)}, f32[512,1152]{1,0:T(8,128)S(1)}, u32[]{:S(2)}, u32[]{:S(2)}) collective-permute-start(f32[512,1152]{1,0:T(8,128)S(1)} %fusion.41), channel_id=1, source_target_pairs={{0,4},{4,8},{8,12},{12,16},{16,20},{20,24},{24,28},{28,32},{32,36}... | collective-permute-start | bytes 7077896 | tf_op jit(solution)/shard_map/ppermute | solution.py:12
  68.0 81.9 %collective-permute-start = (bf16[512,1152]{1,0:T(8,128)(2,1)S(1)}, bf16[512,1152]{1,0:T(8,128)(2,1)S(1)}, u32[]{:S(2)}, u32[]{:S(2)}) collective-permute-start(bf16[512,1152]{1,0:T(8,128)(2,1)S(1)} %multiply_convert_fusion.2), channel_id=1, source_target_pairs={{0,4},{4,8},{8,12},{12,16},{16,20},{20,24},{24,28},{28,32},{32,36}... | collective-permute-start | bytes 3538952 | tf_op jit(solution)/shard_map/ppermute | solution.py:12
  151.8 84.3 %collective-permute-start.4 = (f32[512,1152]{1,0:T(8,128)S(1)}, f32[512,1152]{1,0:T(8,128)S(1)}, u32[]{:S(2)}, u32[]{:S(2)}) collective-permute-start(f32[512,1152]{1,0:T(8,128)S(1)} %convolution_add_fusion), channel_id=1, source_target_pairs={{0,4},{4,8},{8,12},{12,16},{16,20},{20,24},{24,28},{28,32},{32,36}... | collective-permute-start | bytes 7077896 | tf_op jit(solution)/shard_map/ppermute | solution.py:12
  151.9 82.3 %collective-permute-start.1 = (bf16[512,1152]{1,0:T(8,128)(2,1)S(1)}, bf16[512,1152]{1,0:T(8,128)(2,1)S(1)}, u32[]{:S(2)}, u32[]{:S(2)}) collective-permute-start(bf16[512,1152]{1,0:T(8,128)(2,1)S(1)} %collective-permute-done), channel_id=1, source_target_pairs={{0,4},{4,8},{8,12},{12,16},{16,20},{20,24},{24,28},{28,32},{32,36}... | collective-permute-start | bytes 3538952 | tf_op jit(solution)/shard_map/ppermute | solution.py:12
  236.4 83.6 %collective-permute-start.5 = (f32[512,1152]{1,0:T(8,128)S(1)}, f32[512,1152]{1,0:T(8,128)S(1)}, u32[]{:S(2)}, u32[]{:S(2)}) collective-permute-start(f32[512,1152]{1,0:T(8,128)S(1)} %add.99), channel_id=1, source_target_pairs={{0,4},{4,8},{8,12},{12,16},{16,20},{20,24},{24,28},{28,32},{32,36}... | collective-permute-start | bytes 7077896 | tf_op jit(solution)/shard_map/ppermute | solution.py:12
  236.6 81.5 %collective-permute-start.2 = (bf16[512,1152]{1,0:T(8,128)(2,1)S(1)}, bf16[512,1152]{1,0:T(8,128)(2,1)S(1)}, u32[]{:S(2)}, u32[]{:S(2)}) collective-permute-start(bf16[512,1152]{1,0:T(8,128)(2,1)S(1)} %collective-permute-done.1), channel_id=1, source_target_pairs={{0,4},{4,8},{8,12},{12,16},{16,20},{20,24},{24,28},{28,32},{32,36}... | collective-permute-start | bytes 3538952 | tf_op jit(solution)/shard_map/ppermute | solution.py:12
  320.2 91.0 %collective-permute-start.6 = (f32[512,1152]{1,0:T(8,128)S(1)}, f32[512,1152]{1,0:T(8,128)S(1)}, u32[]{:S(2)}, u32[]{:S(2)}) collective-permute-start(f32[512,1152]{1,0:T(8,128)S(1)} %add.100), channel_id=1, source_target_pairs={{0,244},{4,248},{8,252},{12,0},{16,4},{20,8},{24,12},{28,16},{32,2... | collective-permute-start | bytes 7077896 | tf_op jit(solution)/shard_map/ppermute | solution.py:12
  324.4 1.8 copy-start.1
  412.0 1.0 copy-start.2
  499.0 238.8 %copy-start.4 = (u32[256]{0:T(256)S(1)}, u32[256]{0:T(256)}, u32[]{:S(2)}) copy-start(u32[256]{0:T(256)} %constant.28) | copy-start | bytes 3076
  687.3 6.7 collective-permute-start.22
  688.6 6.8 collective-permute-start.21
  690.0 18.4 %collective-permute-start.20 = (f32[288,48]{0,1:T(8,128)S(1)}, f32[288,48]{0,1:T(8,128)S(1)}, u32[]{:S(2)}, u32[]{:S(2)}) collective-permute-start(f32[288,48]{0,1:T(8,128)S(1)} %fusion), channel_id=1, source_target_pairs={{0,56},{4,60},{8,64},{12,68},{16,72},{20,76},{24,80},{28,84},{32,8... | collective-permute-start | bytes 165896
  691.3 19.6 %collective-permute-start.19 = (f32[288,48]{0,1:T(8,128)S(1)}, f32[288,48]{0,1:T(8,128)S(1)}, u32[]{:S(2)}, u32[]{:S(2)}) collective-permute-start(f32[288,48]{0,1:T(8,128)S(1)} %fusion), channel_id=1, source_target_pairs={{0,52},{4,56},{8,60},{12,64},{16,68},{20,72},{24,76},{28,80},{32,8... | collective-permute-start | bytes 165896
  692.6 23.8 %collective-permute-start.18 = (f32[288,48]{0,1:T(8,128)S(1)}, f32[288,48]{0,1:T(8,128)S(1)}, u32[]{:S(2)}, u32[]{:S(2)}) collective-permute-start(f32[288,48]{0,1:T(8,128)S(1)} %fusion), channel_id=1, source_target_pairs={{0,48},{4,52},{8,56},{12,60},{16,64},{20,68},{24,72},{28,76},{32,8... | collective-permute-start | bytes 165896
  694.1 39.5 %copy-start.3 = (f32[288,36]{0,1:T(8,128)}, f32[288,36]{0,1:T(8,128)S(1)}, u32[]{:S(2)}) copy-start(f32[288,36]{0,1:T(8,128)S(1)} %collective-permute-done.22) | copy-start | bytes 124420
  694.1 24.2 %collective-permute-start.17 = (f32[288,48]{0,1:T(8,128)S(1)}, f32[288,48]{0,1:T(8,128)S(1)}, u32[]{:S(2)}, u32[]{:S(2)}) collective-permute-start(f32[288,48]{0,1:T(8,128)S(1)} %fusion), channel_id=1, source_target_pairs={{0,44},{4,48},{8,52},{12,56},{16,60},{20,64},{24,68},{28,72},{32,7... | collective-permute-start | bytes 165896
  695.4 26.5 %collective-permute-start.16 = (f32[288,48]{0,1:T(8,128)S(1)}, f32[288,48]{0,1:T(8,128)S(1)}, u32[]{:S(2)}, u32[]{:S(2)}) collective-permute-start(f32[288,48]{0,1:T(8,128)S(1)} %fusion), channel_id=1, source_target_pairs={{0,40},{4,44},{8,48},{12,52},{16,56},{20,60},{24,64},{28,68},{32,7... | collective-permute-start | bytes 165896
  708.3 17.4 %collective-permute-start.15 = (f32[288,48]{0,1:T(8,128)S(1)}, f32[288,48]{0,1:T(8,128)S(1)}, u32[]{:S(2)}, u32[]{:S(2)}) collective-permute-start(f32[288,48]{0,1:T(8,128)S(1)} %fusion), channel_id=1, source_target_pairs={{0,36},{4,40},{8,44},{12,48},{16,52},{20,56},{24,60},{28,64},{32,6... | collective-permute-start | bytes 165896
  710.9 17.9 %collective-permute-start.14 = (f32[288,48]{0,1:T(8,128)S(1)}, f32[288,48]{0,1:T(8,128)S(1)}, u32[]{:S(2)}, u32[]{:S(2)}) collective-permute-start(f32[288,48]{0,1:T(8,128)S(1)} %fusion), channel_id=1, source_target_pairs={{0,32},{4,36},{8,40},{12,44},{16,48},{20,52},{24,56},{28,60},{32,6... | collective-permute-start | bytes 165896
  716.3 15.8 %collective-permute-start.13 = (f32[288,48]{0,1:T(8,128)S(1)}, f32[288,48]{0,1:T(8,128)S(1)}, u32[]{:S(2)}, u32[]{:S(2)}) collective-permute-start(f32[288,48]{0,1:T(8,128)S(1)} %fusion), channel_id=1, source_target_pairs={{0,28},{4,32},{8,36},{12,40},{16,44},{20,48},{24,52},{28,56},{32,6... | collective-permute-start | bytes 165896
  718.3 15.2 %collective-permute-start.12 = (f32[288,48]{0,1:T(8,128)S(1)}, f32[288,48]{0,1:T(8,128)S(1)}, u32[]{:S(2)}, u32[]{:S(2)}) collective-permute-start(f32[288,48]{0,1:T(8,128)S(1)} %fusion), channel_id=1, source_target_pairs={{0,24},{4,28},{8,32},{12,36},{16,40},{20,44},{24,48},{28,52},{32,5... | collective-permute-start | bytes 165896
  721.9 17.1 %collective-permute-start.11 = (f32[288,48]{0,1:T(8,128)S(1)}, f32[288,48]{0,1:T(8,128)S(1)}, u32[]{:S(2)}, u32[]{:S(2)}) collective-permute-start(f32[288,48]{0,1:T(8,128)S(1)} %fusion), channel_id=1, source_target_pairs={{0,20},{4,24},{8,28},{12,32},{16,36},{20,40},{24,44},{28,48},{32,5... | collective-permute-start | bytes 165896
  725.7 13.3 %collective-permute-start.10 = (f32[288,48]{0,1:T(8,128)S(1)}, f32[288,48]{0,1:T(8,128)S(1)}, u32[]{:S(2)}, u32[]{:S(2)}) collective-permute-start(f32[288,48]{0,1:T(8,128)S(1)} %fusion), channel_id=1, source_target_pairs={{0,16},{4,20},{8,24},{12,28},{16,32},{20,36},{24,40},{28,44},{32,4... | collective-permute-start | bytes 165896
  728.8 10.3 %collective-permute-start.9 = (f32[288,48]{0,1:T(8,128)S(1)}, f32[288,48]{0,1:T(8,128)S(1)}, u32[]{:S(2)}, u32[]{:S(2)}) collective-permute-start(f32[288,48]{0,1:T(8,128)S(1)} %fusion), channel_id=1, source_target_pairs={{0,12},{4,16},{8,20},{12,24},{16,28},{20,32},{24,36},{28,40},{32,4... | collective-permute-start | bytes 165896
  732.1 6.9 collective-permute-start.8
  733.6 6.0 collective-permute-start.7
Sparse Core Ops, SparseCore 0:
  9.8 47.6 all-gather.1
  426.3 68.7 reduce-scatter.5
